TPU v7x, 256 devices: a whole 4x4x8 slice. The times are simulated.
256 devices in a mesh: section: 8 (over z), tm: 32 (over x, y, core).
Axes of the slice: x: 4, y: 4, z: 8, core: 2. Of those that a mesh axis runs over, the one named last changes fastest.
Arguments:
- acts: bfloat16 [8, 2, 2048, 1024], P('section', None, 'tm'), may hold values from -600 to 600
- grad_top: bfloat16 [2, 2048, 1024], P(None, 'tm'), may hold values from -6 to 6
- w_in: bfloat16 [8, 1024, 3072], P('section'), may hold values from -0.1875 to 0.1875
- w_out: bfloat16 [8, 1024, 1024], P('section'), may hold values from -0.1875 to 0.1875
- offsets: int32 [32, 5], P('tm'), may hold values from 0 to 16, as said below
Outputs:
- d_acts: bfloat16 [8, 2, 2048, 1024], P('section', None, 'tm')
- d_w_in: float32 [8, 1024, 3072], P('section', 'tm')
- d_w_out: float32 [8, 1024, 1024], P('section', 'tm')
Inputs may be any that keep to these rules, and one draw needn't show every extreme that they name: offsets[t, k] is 0 or 2**k, and 0 wherever t < 2**k; the last shard uses every level.
All inputs are finite; a program needn't handle non-finite values.
Results may differ from a plain program's by a relative error of at most 0.018.
The roundings to bfloat16 on the way count: a program that leaves them out, or rounds other values in their place, can miss the bound.
Values may be sent and summed in bfloat16 or wider, within the bound.
A program may use at most 128 MiB of HBM per device.

v0:
```python
import jax
import jax.numpy as jnp
from jax import lax
from jax.sharding import PartitionSpec as P

HEAD_DIM = 64
epsilon = 1e-06
negative_fill = -1e30


def shifted(value, axis, steps):
    count = lax.axis_size(axis)
    initial, last = (max(0, -steps), min(count, count - steps))
    return lax.ppermute(value, axis, [(source, source + steps) for source in range(initial, last)])


def normalize(inputs):
    values = inputs.astype(jnp.float32)
    inverse_rms = lax.rsqrt(jnp.mean(values * values, axis=-1, keepdims=True) + epsilon)
    return (values * inverse_rms, inverse_rms)


def key_bias(level_flags, shard_rows):
    position = jnp.arange(shard_rows)
    own_part = position[None, :] <= position[:, None]
    far_part = jnp.repeat(level_flags != 0, shard_rows)
    far_part = jnp.broadcast_to(far_part[None, :], (shard_rows, far_part.shape[0]))
    return jnp.concatenate([own_part, far_part], 1)


def split_heads(row_block):
    return row_block.reshape(row_block.shape[0], -1, HEAD_DIM)


def softmax_keys(queries, key_heads, allowed):
    scores = jnp.einsum(
        "ihd,jhd->hij", queries, key_heads, preferred_element_type=jnp.float32
    ) * HEAD_DIM ** (-0.5)
    scores = jnp.where(allowed[None], scores, negative_fill)
    highest = jnp.max(scores, axis=-1, keepdims=True)
    shifted_exp = jnp.where(allowed[None], jnp.exp(scores - highest), 0.0)
    return shifted_exp / jnp.sum(shifted_exp, axis=-1, keepdims=True)


def attend(query_rows, key_rows, allowed):
    model_width = query_rows.shape[1]
    probability = softmax_keys(
        split_heads(query_rows), split_heads(key_rows[:, :model_width]), allowed
    )
    attended = jnp.einsum(
        "hij,jhd->ihd",
        probability.astype(jnp.bfloat16),
        split_heads(key_rows[:, model_width:]),
        preferred_element_type=jnp.float32,
    )
    return attended.reshape(query_rows.shape).astype(jnp.bfloat16)


def attend_back(query_rows, key_rows, allowed, incoming, attended, w_proj):
    model_width = query_rows.shape[1]
    queries = split_heads(query_rows)
    key_heads = split_heads(key_rows[:, :model_width])
    value_heads = split_heads(key_rows[:, model_width:])
    probability = softmax_keys(queries, key_heads, allowed)
    rounded = probability.astype(jnp.bfloat16)
    upstream = lax.dot_general(
        incoming, w_proj, (((1,), (1,)), ((), ())), preferred_element_type=jnp.float32
    ).astype(jnp.bfloat16)
    up_heads = split_heads(upstream)
    delta = jnp.einsum(
        "ihd,ihd->hi", up_heads.astype(jnp.float32), split_heads(attended).astype(jnp.float32)
    )[..., None]
    prob_grad = jnp.einsum(
        "ihd,jhd->hij", up_heads, value_heads, preferred_element_type=jnp.float32
    )
    score_grad = (probability * (prob_grad - delta)).astype(jnp.bfloat16)
    scale_factor = HEAD_DIM ** (-0.5)
    query_grad = (
        jnp.einsum("hij,jhd->ihd", score_grad, key_heads, preferred_element_type=jnp.float32)
        * scale_factor
    )
    key_grad = (
        jnp.einsum("hij,ihd->jhd", score_grad, queries, preferred_element_type=jnp.float32)
        * scale_factor
    )
    value_grad = jnp.einsum("hij,ihd->jhd", rounded, up_heads, preferred_element_type=jnp.float32)
    return (
        query_grad.reshape(-1, model_width),
        key_grad.reshape(-1, model_width),
        value_grad.reshape(-1, model_width),
    )


def per_device(acts, grad_top, w_in, w_out, offsets):
    sections = lax.axis_size("section")
    shards = lax.axis_size("tm")
    levels = shards.bit_length() - 1
    section_index = lax.axis_index("section")
    micro_count = acts.shape[1]
    shard_rows = acts.shape[2]
    model_width = acts.shape[3]
    w_qkv = w_in[0]
    w_proj = w_out[0]
    level_flags = offsets[0]
    normed, inverse_rms = normalize(acts[0])
    rounded_norm = normed.astype(jnp.bfloat16)
    qkv = jnp.dot(rounded_norm.reshape(-1, model_width), w_qkv, preferred_element_type=jnp.float32)
    qkv = qkv.astype(jnp.bfloat16).reshape(micro_count, shard_rows, 3 * model_width)
    pairs = qkv[..., model_width:]
    every_pair = lax.all_gather(pairs, "tm", axis=1, tiled=True)
    shard_index = lax.axis_index("tm")
    far_list = []
    for level in range(levels):
        source = jnp.maximum(shard_index - 2**level, 0) * shard_rows
        far_list.append(lax.dynamic_slice_in_dim(every_pair, source, shard_rows, 1))
    key_rows = jnp.concatenate([pairs] + far_list, 1)
    allowed = key_bias(level_flags, shard_rows)
    attended = jnp.stack(
        [
            attend(qkv[index, :, :model_width], key_rows[index], allowed)
            for index in range(micro_count)
        ],
        0,
    )

    def attention_part(incoming, slot):
        query_rows = lax.dynamic_index_in_dim(qkv, slot, 0, False)[:, :model_width]
        slot_keys = lax.dynamic_index_in_dim(key_rows, slot, 0, False)
        slot_attended = lax.dynamic_index_in_dim(attended, slot, 0, False)
        query_grad, key_grad, value_grad = attend_back(
            query_rows, slot_keys, allowed, incoming, slot_attended, w_proj
        )
        owner_sum = jnp.concatenate([key_grad[:shard_rows], value_grad[:shard_rows]], 1)
        far_part = jnp.concatenate([key_grad[shard_rows:], value_grad[shard_rows:]], 1)
        far_part = far_part.astype(jnp.bfloat16).reshape(levels, shard_rows, 2 * model_width)
        return (query_grad, owner_sum, far_part)

    def empty_attention(incoming, slot):
        return (
            jnp.zeros((shard_rows, model_width), jnp.float32),
            jnp.zeros((shard_rows, 2 * model_width), jnp.float32),
            jnp.zeros((levels, shard_rows, 2 * model_width), jnp.bfloat16),
        )

    def norm_part(qkv_grad, incoming, slot):
        norm_grad = lax.dot_general(
            qkv_grad, w_qkv, (((1,), (1,)), ((), ())), preferred_element_type=jnp.float32
        )
        slot_normed = lax.dynamic_index_in_dim(normed, slot, 0, False)
        slot_rms = lax.dynamic_index_in_dim(inverse_rms, slot, 0, False)
        inner = jnp.mean(norm_grad * slot_normed, axis=-1, keepdims=True)
        return (incoming.astype(jnp.float32) + slot_rms * (norm_grad - slot_normed * inner)).astype(
            jnp.bfloat16
        )

    def empty_norm(qkv_grad, incoming, slot):
        return jnp.zeros((shard_rows, model_width), jnp.bfloat16)

    def step(turn, carry):
        received, grad_store, qkv_store, incoming_store = carry
        slot_raw = turn - (sections - 1 - section_index)
        active = (slot_raw >= 0) & (slot_raw < micro_count)
        slot = jnp.clip(slot_raw, 0, micro_count - 1)
        incoming = jnp.where(
            section_index == sections - 1,
            lax.dynamic_index_in_dim(grad_top, slot, 0, False),
            received,
        )
        query_grad, owner_sum, far_part = lax.cond(
            active, attention_part, empty_attention, incoming, slot
        )
        for level in range(levels):
            owner_sum = owner_sum + shifted(far_part[level], "tm", -(2**level)).astype(jnp.float32)
        qkv_grad = jnp.concatenate([query_grad, owner_sum], 1).astype(jnp.bfloat16)
        grad_in = lax.cond(active, norm_part, empty_norm, qkv_grad, incoming, slot)
        sent_down = shifted(grad_in, "section", -1)
        grad_store = jnp.where(
            active, lax.dynamic_update_index_in_dim(grad_store, grad_in, slot, 0), grad_store
        )
        qkv_store = jnp.where(
            active, lax.dynamic_update_index_in_dim(qkv_store, qkv_grad, slot, 0), qkv_store
        )
        incoming_store = jnp.where(
            active,
            lax.dynamic_update_index_in_dim(incoming_store, incoming, slot, 0),
            incoming_store,
        )
        return (sent_down, grad_store, qkv_store, incoming_store)

    initial = (
        jnp.zeros((shard_rows, model_width), jnp.bfloat16),
        jnp.zeros((micro_count, shard_rows, model_width), jnp.bfloat16),
        jnp.zeros((micro_count, shard_rows, 3 * model_width), jnp.bfloat16),
        jnp.zeros((micro_count, shard_rows, model_width), jnp.bfloat16),
    )
    received, grad_store, qkv_store, incoming_store = lax.fori_loop(
        0, sections + micro_count - 1, step, initial
    )
    flat_norm = rounded_norm.reshape(-1, model_width)
    flat_attended = attended.reshape(-1, model_width)
    flat_qkv = qkv_store.reshape(-1, 3 * model_width)
    flat_incoming = incoming_store.reshape(-1, model_width)
    contract = (((0,), (0,)), ((), ()))
    first = lax.dot_general(flat_norm, flat_qkv, contract, preferred_element_type=jnp.float32)
    second = lax.dot_general(
        flat_attended, flat_incoming, contract, preferred_element_type=jnp.float32
    )
    summed = lax.psum_scatter(
        jnp.concatenate([first, second], 1).astype(jnp.bfloat16),
        "tm",
        scatter_dimension=0,
        tiled=True,
    ).astype(jnp.float32)
    return (
        grad_store[None],
        summed[None, :, : 3 * model_width],
        summed[None, :, 3 * model_width :],
    )


def solution(mesh):
    placed = (
        P("section", None, "tm", None),
        P(None, "tm", None),
        P("section", None, None),
        P("section", None, None),
        P("tm", None),
    )
    return jax.shard_map(
        per_device,
        mesh=mesh,
        in_specs=placed,
        out_specs=(
            P("section", None, "tm", None),
            P("section", "tm", None),
            P("section", "tm", None),
        ),
        check_vma=False,
    )
```

profile of v0, /device:TPU:2, one launch (start us, length us, event | category | flops | bytes accessed | tf_op | source)
XLA Modules:
  0.0 832.1 jit_solution(8413737208100853493)
XLA Ops:
  9.4 3.8 convolution_convert_fusion.1
  16.6 78.4 %all-gather.2.cloned.1.call-done = bf16[2,2048,2048]{2,1,0:T(8,128)(2,1)} async-done(((bf16[2,64,2048]{2,1,0:T(8,128)(2,1)}), bf16[2,2048,2048]{2,1,0:T(8,128)(2,1)}) %all-gather.2.cloned.1.call-update) | async-done | bytes 16777232 | tf_op jit(solution)/shard_map/all_gather | solution.py:110
  104.5 3.5 slice_bitcast_fusion.6
  108.0 4.6 copy.45
  132.7 568.1 %while.21 = (s32[]{:T(128)}, bf16[64,1024]{1,0:T(8,128)(2,1)}, bf16[2,64,1024]{2,1,0:T(8,128)(2,1)}, bf16[2,64,3072]{2,1,0:T(8,128)(2,1)}, bf16[2,64,1024]{2,1,0...) while((s32[]{:T(128)}, bf16[64,1024]{1,0:T(8,128)(2,1)}, ...), condition=%wide.region_13.14_spmd, body=%wide.region_5.13_spmd.sunk | while | flops 800390528 | bytes 100328176 | solution.py:196
  139.4 3.3 collective-permute-start.2
  148.2 4.9 collective-permute-done.1
  153.2 5.3 collective-permute-done.3
  166.7 3.7 collective-permute-done.5
  183.3 3.9 collective-permute-done
  187.2 3.8 collective-permute-done.1
  191.0 3.4 collective-permute-done.3
  203.4 3.2 collective-permute-done.5
  220.0 4.4 collective-permute-done
  224.4 3.8 collective-permute-done.1
  239.3 3.6 collective-permute-done.5
  255.9 3.2 collective-permute-done
  259.1 5.5 collective-permute-done.1
  275.9 3.8 collective-permute-done.5
  289.7 3.1 collective-permute-start.4
  292.8 3.3 collective-permute-done
  296.2 5.3 collective-permute-done.1
  312.8 3.2 collective-permute-done.5
  324.0 3.1 collective-permute-start.3
  327.1 3.3 collective-permute-start.4
  330.4 3.9 collective-permute-done
  334.2 5.5 collective-permute-done.1
  348.6 4.8 collective-permute-done.5
  361.5 3.1 collective-permute-start.3
  364.6 3.3 collective-permute-start.4
  367.9 4.0 collective-permute-done
  371.9 5.9 collective-permute-done.1
  385.1 189.5 %collective-permute-done.5 = bf16[64,1024]{1,0:T(8,128)(2,1)} collective-permute-done((bf16[64,1024]{1,0:T(8,128)(2,1)}, bf16[64,1024]{1,0:T(8,128)(2,1)}, u32[]{:S(2)}, u32[]{:S(2)}) %collective-permute-start.5) | collective-permute-done | bytes 131104 | tf_op jit(solution)/shard_map/while/body/eval_jaxpr/ppermute | solution.py:14
  576.3 22.1 %conditional.4 = (bf16[5,64,2048]{2,1,0:T(8,128)(2,1)S(1)}, f32[64,2048]{1,0:T(8,128)}, bf16[64,1024]{1,0:T(8,128)(2,1)S(1)}, bf16[1,64,1024]{2,1,0:T(8,128)(2,1)S(1)}) conditional(s32[]{:T(128)} %convert_element_type.218, () %tuple.93, (s32[]{:T(128)}, bf16[2,384,2048]{1,2,0:T(8,128)(2,1)}, pred[64,384]{1,0:T(8,128)(4,1)}, ...), branch_computations={%region_6.6_spmd, %region_7.9_spmd} | conditional | flops 393805184 | bytes 68079920 | solution.py:169
  606.8 3.3 collective-permute-start.4
  610.1 4.3 collective-permute-done
  614.4 5.5 collective-permute-done.1
  622.9 6.8 conditional.5
  622.9 5.1 fusion
  638.7 22.1 %conditional.4 = (bf16[5,64,2048]{2,1,0:T(8,128)(2,1)S(1)}, f32[64,2048]{1,0:T(8,128)}, bf16[64,1024]{1,0:T(8,128)(2,1)S(1)}, bf16[1,64,1024]{2,1,0:T(8,128)(2,1)S(1)}) conditional(s32[]{:T(128)} %convert_element_type.218, () %tuple.93, (s32[]{:T(128)}, bf16[2,384,2048]{1,2,0:T(8,128)(2,1)}, pred[64,384]{1,0:T(8,128)(4,1)}, ...), branch_computations={%region_6.6_spmd, %region_7.9_spmd} | conditional | flops 393805184 | bytes 68079920 | solution.py:169
  666.1 3.1 collective-permute-start.3
  672.2 7.2 collective-permute-done
  679.5 5.6 collective-permute-done.1
  686.4 6.8 conditional.5
  686.4 5.1 fusion
  700.8 5.9 bitcast_convert_fusion
  708.3 6.9 pad_maximum_fusion.3
  715.2 107.6 %reduce-scatter.2.cloned.1.call-done = bf16[32,4096]{1,0:T(8,128)(2,1)} async-done(((bf16[1024,4096]{1,0:T(8,128)(2,1)}), bf16[32,4096]{1,0:T(8,128)(2,1)}) %reduce-scatter.2.cloned.1.call-update) | async-done | bytes 262160 | tf_op jit(solution)/shard_map/reduce_scatter | solution.py:208
  (369 shorter events, 281.2 us)
Async XLA Ops:
  7.2 87.9 %all-gather.2.cloned.1.call-start = ((), (), s32[]{:S(2)}) async-start(), calls=%async_computation.1 | async-start | bytes 17301504 | tf_op jit(solution)/shard_map/all_gather | solution.py:110
  14.3 808.5 %reduce-scatter.2.cloned.1.call-start = ((), (), s32[]{:S(2)}) async-start(), calls=%async_computation.2 | async-start | bytes 8650752 | tf_op jit(solution)/shard_map/reduce_scatter | solution.py:208
  135.6 12.6 %collective-permute-start = (bf16[64,2048]{1,0:T(8,128)(2,1)S(1)}, bf16[64,2048]{1,0:T(8,128)(2,1)S(1)}, u32[]{:S(2)}, u32[]{:S(2)}) collective-permute-start(bf16[64,2048]{1,0:T(8,128)(2,1)S(1)} %get-tuple-element.614), channel_id=1, source_target_pairs={{16,0},{17,1},{18,2},{19,3},{20,4},{21,5},{22,6},{23,7},{24,8},{25... | collective-permute-start | bytes 786440 | tf_op jit(solution)/shard_map/while/body/eval_jaxpr/ppermute | solution.py:14
  136.9 16.2 %collective-permute-start.1 = (bf16[64,2048]{1,0:T(8,128)(2,1)S(1)}, bf16[64,2048]{1,0:T(8,128)(2,1)S(1)}, u32[]{:S(2)}, u32[]{:S(2)}) collective-permute-start(bf16[64,2048]{1,0:T(8,128)(2,1)S(1)} %get-tuple-element.615), channel_id=1, source_target_pairs={{8,0},{9,1},{10,2},{11,3},{12,4},{13,5},{14,6},{15,7},{16,8},{17,9... | collective-permute-start | bytes 786440 | tf_op jit(solution)/shard_map/while/body/eval_jaxpr/ppermute | solution.py:14
  139.4 13.8 %collective-permute-start.2 = (bf16[64,2048]{1,0:T(8,128)(2,1)S(1)}, bf16[64,2048]{1,0:T(8,128)(2,1)S(1)}, u32[]{:S(2)}, u32[]{:S(2)}) collective-permute-start(bf16[64,2048]{1,0:T(8,128)(2,1)S(1)} %get-tuple-element.616), channel_id=1, source_target_pairs={{4,0},{5,1},{6,2},{7,3},{8,4},{9,5},{10,6},{11,7},{12,8},{13,9},{1... | collective-permute-start | bytes 786440 | tf_op jit(solution)/shard_map/while/body/eval_jaxpr/ppermute | solution.py:14
  142.7 15.7 %collective-permute-start.3 = (bf16[64,2048]{1,0:T(8,128)(2,1)S(1)}, bf16[64,2048]{1,0:T(8,128)(2,1)S(1)}, u32[]{:S(2)}, u32[]{:S(2)}) collective-permute-start(bf16[64,2048]{1,0:T(8,128)(2,1)S(1)} %get-tuple-element.617), channel_id=1, source_target_pairs={{2,0},{3,1},{4,2},{5,3},{6,4},{7,5},{8,6},{9,7},{10,8},{11,9},{12,... | collective-permute-start | bytes 786440 | tf_op jit(solution)/shard_map/while/body/eval_jaxpr/ppermute | solution.py:14
  145.8 14.2 %collective-permute-start.4 = (bf16[64,2048]{1,0:T(8,128)(2,1)S(1)}, bf16[64,2048]{1,0:T(8,128)(2,1)S(1)}, u32[]{:S(2)}, u32[]{:S(2)}) collective-permute-start(bf16[64,2048]{1,0:T(8,128)(2,1)S(1)} %get-tuple-element.619), channel_id=1, source_target_pairs={{1,0},{2,1},{3,2},{4,3},{5,4},{6,5},{7,6},{8,7},{9,8},{10,9},{11,1... | collective-permute-start | bytes 786440 | tf_op jit(solution)/shard_map/while/body/eval_jaxpr/ppermute | solution.py:14
  173.3 13.9 %collective-permute-start = (bf16[64,2048]{1,0:T(8,128)(2,1)S(1)}, bf16[64,2048]{1,0:T(8,128)(2,1)S(1)}, u32[]{:S(2)}, u32[]{:S(2)}) collective-permute-start(bf16[64,2048]{1,0:T(8,128)(2,1)S(1)} %get-tuple-element.614), channel_id=1, source_target_pairs={{16,0},{17,1},{18,2},{19,3},{20,4},{21,5},{22,6},{23,7},{24,8},{25... | collective-permute-start | bytes 786440 | tf_op jit(solution)/shard_map/while/body/eval_jaxpr/ppermute | solution.py:14
  174.6 16.4 %collective-permute-start.1 = (bf16[64,2048]{1,0:T(8,128)(2,1)S(1)}, bf16[64,2048]{1,0:T(8,128)(2,1)S(1)}, u32[]{:S(2)}, u32[]{:S(2)}) collective-permute-start(bf16[64,2048]{1,0:T(8,128)(2,1)S(1)} %get-tuple-element.615), channel_id=1, source_target_pairs={{8,0},{9,1},{10,2},{11,3},{12,4},{13,5},{14,6},{15,7},{16,8},{17,9... | collective-permute-start | bytes 786440 | tf_op jit(solution)/shard_map/while/body/eval_jaxpr/ppermute | solution.py:14
  176.5 14.4 %collective-permute-start.2 = (bf16[64,2048]{1,0:T(8,128)(2,1)S(1)}, bf16[64,2048]{1,0:T(8,128)(2,1)S(1)}, u32[]{:S(2)}, u32[]{:S(2)}) collective-permute-start(bf16[64,2048]{1,0:T(8,128)(2,1)S(1)} %get-tuple-element.616), channel_id=1, source_target_pairs={{4,0},{5,1},{6,2},{7,3},{8,4},{9,5},{10,6},{11,7},{12,8},{13,9},{1... | collective-permute-start | bytes 786440 | tf_op jit(solution)/shard_map/while/body/eval_jaxpr/ppermute | solution.py:14
  178.5 16.0 %collective-permute-start.3 = (bf16[64,2048]{1,0:T(8,128)(2,1)S(1)}, bf16[64,2048]{1,0:T(8,128)(2,1)S(1)}, u32[]{:S(2)}, u32[]{:S(2)}) collective-permute-start(bf16[64,2048]{1,0:T(8,128)(2,1)S(1)} %get-tuple-element.617), channel_id=1, source_target_pairs={{2,0},{3,1},{4,2},{5,3},{6,4},{7,5},{8,6},{9,7},{10,8},{11,9},{12,... | collective-permute-start | bytes 786440 | tf_op jit(solution)/shard_map/while/body/eval_jaxpr/ppermute | solution.py:14
  180.4 16.3 %collective-permute-start.4 = (bf16[64,2048]{1,0:T(8,128)(2,1)S(1)}, bf16[64,2048]{1,0:T(8,128)(2,1)S(1)}, u32[]{:S(2)}, u32[]{:S(2)}) collective-permute-start(bf16[64,2048]{1,0:T(8,128)(2,1)S(1)} %get-tuple-element.619), channel_id=1, source_target_pairs={{1,0},{2,1},{3,2},{4,3},{5,4},{6,5},{7,6},{8,7},{9,8},{10,9},{11,1... | collective-permute-start | bytes 786440 | tf_op jit(solution)/shard_map/while/body/eval_jaxpr/ppermute | solution.py:14
  209.5 14.9 %collective-permute-start = (bf16[64,2048]{1,0:T(8,128)(2,1)S(1)}, bf16[64,2048]{1,0:T(8,128)(2,1)S(1)}, u32[]{:S(2)}, u32[]{:S(2)}) collective-permute-start(bf16[64,2048]{1,0:T(8,128)(2,1)S(1)} %get-tuple-element.614), channel_id=1, source_target_pairs={{16,0},{17,1},{18,2},{19,3},{20,4},{21,5},{22,6},{23,7},{24,8},{25... | collective-permute-start | bytes 786440 | tf_op jit(solution)/shard_map/while/body/eval_jaxpr/ppermute | solution.py:14
  210.8 17.4 %collective-permute-start.1 = (bf16[64,2048]{1,0:T(8,128)(2,1)S(1)}, bf16[64,2048]{1,0:T(8,128)(2,1)S(1)}, u32[]{:S(2)}, u32[]{:S(2)}) collective-permute-start(bf16[64,2048]{1,0:T(8,128)(2,1)S(1)} %get-tuple-element.615), channel_id=1, source_target_pairs={{8,0},{9,1},{10,2},{11,3},{12,4},{13,5},{14,6},{15,7},{16,8},{17,9... | collective-permute-start | bytes 786440 | tf_op jit(solution)/shard_map/while/body/eval_jaxpr/ppermute | solution.py:14
  212.8 15.5 %collective-permute-start.2 = (bf16[64,2048]{1,0:T(8,128)(2,1)S(1)}, bf16[64,2048]{1,0:T(8,128)(2,1)S(1)}, u32[]{:S(2)}, u32[]{:S(2)}) collective-permute-start(bf16[64,2048]{1,0:T(8,128)(2,1)S(1)} %get-tuple-element.616), channel_id=1, source_target_pairs={{4,0},{5,1},{6,2},{7,3},{8,4},{9,5},{10,6},{11,7},{12,8},{13,9},{1... | collective-permute-start | bytes 786440 | tf_op jit(solution)/shard_map/while/body/eval_jaxpr/ppermute | solution.py:14
  214.7 15.0 %collective-permute-start.3 = (bf16[64,2048]{1,0:T(8,128)(2,1)S(1)}, bf16[64,2048]{1,0:T(8,128)(2,1)S(1)}, u32[]{:S(2)}, u32[]{:S(2)}) collective-permute-start(bf16[64,2048]{1,0:T(8,128)(2,1)S(1)} %get-tuple-element.617), channel_id=1, source_target_pairs={{2,0},{3,1},{4,2},{5,3},{6,4},{7,5},{8,6},{9,7},{10,8},{11,9},{12,... | collective-permute-start | bytes 786440 | tf_op jit(solution)/shard_map/while/body/eval_jaxpr/ppermute | solution.py:14
  217.0 15.6 %collective-permute-start.4 = (bf16[64,2048]{1,0:T(8,128)(2,1)S(1)}, bf16[64,2048]{1,0:T(8,128)(2,1)S(1)}, u32[]{:S(2)}, u32[]{:S(2)}) collective-permute-start(bf16[64,2048]{1,0:T(8,128)(2,1)S(1)} %get-tuple-element.619), channel_id=1, source_target_pairs={{1,0},{2,1},{3,2},{4,3},{5,4},{6,5},{7,6},{8,7},{9,8},{10,9},{11,1... | collective-permute-start | bytes 786440 | tf_op jit(solution)/shard_map/while/body/eval_jaxpr/ppermute | solution.py:14
  245.8 13.3 %collective-permute-start = (bf16[64,2048]{1,0:T(8,128)(2,1)S(1)}, bf16[64,2048]{1,0:T(8,128)(2,1)S(1)}, u32[]{:S(2)}, u32[]{:S(2)}) collective-permute-start(bf16[64,2048]{1,0:T(8,128)(2,1)S(1)} %get-tuple-element.614), channel_id=1, source_target_pairs={{16,0},{17,1},{18,2},{19,3},{20,4},{21,5},{22,6},{23,7},{24,8},{25... | collective-permute-start | bytes 786440 | tf_op jit(solution)/shard_map/while/body/eval_jaxpr/ppermute | solution.py:14
  247.1 17.5 %collective-permute-start.1 = (bf16[64,2048]{1,0:T(8,128)(2,1)S(1)}, bf16[64,2048]{1,0:T(8,128)(2,1)S(1)}, u32[]{:S(2)}, u32[]{:S(2)}) collective-permute-start(bf16[64,2048]{1,0:T(8,128)(2,1)S(1)} %get-tuple-element.615), channel_id=1, source_target_pairs={{8,0},{9,1},{10,2},{11,3},{12,4},{13,5},{14,6},{15,7},{16,8},{17,9... | collective-permute-start | bytes 786440 | tf_op jit(solution)/shard_map/while/body/eval_jaxpr/ppermute | solution.py:14
  249.0 15.6 %collective-permute-start.2 = (bf16[64,2048]{1,0:T(8,128)(2,1)S(1)}, bf16[64,2048]{1,0:T(8,128)(2,1)S(1)}, u32[]{:S(2)}, u32[]{:S(2)}) collective-permute-start(bf16[64,2048]{1,0:T(8,128)(2,1)S(1)} %get-tuple-element.616), channel_id=1, source_target_pairs={{4,0},{5,1},{6,2},{7,3},{8,4},{9,5},{10,6},{11,7},{12,8},{13,9},{1... | collective-permute-start | bytes 786440 | tf_op jit(solution)/shard_map/while/body/eval_jaxpr/ppermute | solution.py:14
  250.9 15.4 %collective-permute-start.3 = (bf16[64,2048]{1,0:T(8,128)(2,1)S(1)}, bf16[64,2048]{1,0:T(8,128)(2,1)S(1)}, u32[]{:S(2)}, u32[]{:S(2)}) collective-permute-start(bf16[64,2048]{1,0:T(8,128)(2,1)S(1)} %get-tuple-element.617), channel_id=1, source_target_pairs={{2,0},{3,1},{4,2},{5,3},{6,4},{7,5},{8,6},{9,7},{10,8},{11,9},{12,... | collective-permute-start | bytes 786440 | tf_op jit(solution)/shard_map/while/body/eval_jaxpr/ppermute | solution.py:14
  252.9 16.3 %collective-permute-start.4 = (bf16[64,2048]{1,0:T(8,128)(2,1)S(1)}, bf16[64,2048]{1,0:T(8,128)(2,1)S(1)}, u32[]{:S(2)}, u32[]{:S(2)}) collective-permute-start(bf16[64,2048]{1,0:T(8,128)(2,1)S(1)} %get-tuple-element.619), channel_id=1, source_target_pairs={{1,0},{2,1},{3,2},{4,3},{5,4},{6,5},{7,6},{8,7},{9,8},{10,9},{11,1... | collective-permute-start | bytes 786440 | tf_op jit(solution)/shard_map/while/body/eval_jaxpr/ppermute | solution.py:14
  282.6 13.5 %collective-permute-start = (bf16[64,2048]{1,0:T(8,128)(2,1)S(1)}, bf16[64,2048]{1,0:T(8,128)(2,1)S(1)}, u32[]{:S(2)}, u32[]{:S(2)}) collective-permute-start(bf16[64,2048]{1,0:T(8,128)(2,1)S(1)} %get-tuple-element.614), channel_id=1, source_target_pairs={{16,0},{17,1},{18,2},{19,3},{20,4},{21,5},{22,6},{23,7},{24,8},{25... | collective-permute-start | bytes 786440 | tf_op jit(solution)/shard_map/while/body/eval_jaxpr/ppermute | solution.py:14
  283.9 17.5 %collective-permute-start.1 = (bf16[64,2048]{1,0:T(8,128)(2,1)S(1)}, bf16[64,2048]{1,0:T(8,128)(2,1)S(1)}, u32[]{:S(2)}, u32[]{:S(2)}) collective-permute-start(bf16[64,2048]{1,0:T(8,128)(2,1)S(1)} %get-tuple-element.615), channel_id=1, source_target_pairs={{8,0},{9,1},{10,2},{11,3},{12,4},{13,5},{14,6},{15,7},{16,8},{17,9... | collective-permute-start | bytes 786440 | tf_op jit(solution)/shard_map/while/body/eval_jaxpr/ppermute | solution.py:14
  285.9 15.6 %collective-permute-start.2 = (bf16[64,2048]{1,0:T(8,128)(2,1)S(1)}, bf16[64,2048]{1,0:T(8,128)(2,1)S(1)}, u32[]{:S(2)}, u32[]{:S(2)}) collective-permute-start(bf16[64,2048]{1,0:T(8,128)(2,1)S(1)} %get-tuple-element.616), channel_id=1, source_target_pairs={{4,0},{5,1},{6,2},{7,3},{8,4},{9,5},{10,6},{11,7},{12,8},{13,9},{1... | collective-permute-start | bytes 786440 | tf_op jit(solution)/shard_map/while/body/eval_jaxpr/ppermute | solution.py:14
  287.8 15.4 %collective-permute-start.3 = (bf16[64,2048]{1,0:T(8,128)(2,1)S(1)}, bf16[64,2048]{1,0:T(8,128)(2,1)S(1)}, u32[]{:S(2)}, u32[]{:S(2)}) collective-permute-start(bf16[64,2048]{1,0:T(8,128)(2,1)S(1)} %get-tuple-element.617), channel_id=1, source_target_pairs={{2,0},{3,1},{4,2},{5,3},{6,4},{7,5},{8,6},{9,7},{10,8},{11,9},{12,... | collective-permute-start | bytes 786440 | tf_op jit(solution)/shard_map/while/body/eval_jaxpr/ppermute | solution.py:14
  289.7 16.3 %collective-permute-start.4 = (bf16[64,2048]{1,0:T(8,128)(2,1)S(1)}, bf16[64,2048]{1,0:T(8,128)(2,1)S(1)}, u32[]{:S(2)}, u32[]{:S(2)}) collective-permute-start(bf16[64,2048]{1,0:T(8,128)(2,1)S(1)} %get-tuple-element.619), channel_id=1, source_target_pairs={{1,0},{2,1},{3,2},{4,3},{5,4},{6,5},{7,6},{8,7},{9,8},{10,9},{11,1... | collective-permute-start | bytes 786440 | tf_op jit(solution)/shard_map/while/body/eval_jaxpr/ppermute | solution.py:14
  318.9 15.4 %collective-permute-start = (bf16[64,2048]{1,0:T(8,128)(2,1)S(1)}, bf16[64,2048]{1,0:T(8,128)(2,1)S(1)}, u32[]{:S(2)}, u32[]{:S(2)}) collective-permute-start(bf16[64,2048]{1,0:T(8,128)(2,1)S(1)} %get-tuple-element.614), channel_id=1, source_target_pairs={{16,0},{17,1},{18,2},{19,3},{20,4},{21,5},{22,6},{23,7},{24,8},{25... | collective-permute-start | bytes 786440 | tf_op jit(solution)/shard_map/while/body/eval_jaxpr/ppermute | solution.py:14
  320.2 19.5 %collective-permute-start.1 = (bf16[64,2048]{1,0:T(8,128)(2,1)S(1)}, bf16[64,2048]{1,0:T(8,128)(2,1)S(1)}, u32[]{:S(2)}, u32[]{:S(2)}) collective-permute-start(bf16[64,2048]{1,0:T(8,128)(2,1)S(1)} %get-tuple-element.615), channel_id=1, source_target_pairs={{8,0},{9,1},{10,2},{11,3},{12,4},{13,5},{14,6},{15,7},{16,8},{17,9... | collective-permute-start | bytes 786440 | tf_op jit(solution)/shard_map/while/body/eval_jaxpr/ppermute | solution.py:14
  322.1 17.6 %collective-permute-start.2 = (bf16[64,2048]{1,0:T(8,128)(2,1)S(1)}, bf16[64,2048]{1,0:T(8,128)(2,1)S(1)}, u32[]{:S(2)}, u32[]{:S(2)}) collective-permute-start(bf16[64,2048]{1,0:T(8,128)(2,1)S(1)} %get-tuple-element.616), channel_id=1, source_target_pairs={{4,0},{5,1},{6,2},{7,3},{8,4},{9,5},{10,6},{11,7},{12,8},{13,9},{1... | collective-permute-start | bytes 786440 | tf_op jit(solution)/shard_map/while/body/eval_jaxpr/ppermute | solution.py:14
  324.0 15.7 %collective-permute-start.3 = (bf16[64,2048]{1,0:T(8,128)(2,1)S(1)}, bf16[64,2048]{1,0:T(8,128)(2,1)S(1)}, u32[]{:S(2)}, u32[]{:S(2)}) collective-permute-start(bf16[64,2048]{1,0:T(8,128)(2,1)S(1)} %get-tuple-element.617), channel_id=1, source_target_pairs={{2,0},{3,1},{4,2},{5,3},{6,4},{7,5},{8,6},{9,7},{10,8},{11,9},{12,... | collective-permute-start | bytes 786440 | tf_op jit(solution)/shard_map/while/body/eval_jaxpr/ppermute | solution.py:14
  327.1 14.8 %collective-permute-start.4 = (bf16[64,2048]{1,0:T(8,128)(2,1)S(1)}, bf16[64,2048]{1,0:T(8,128)(2,1)S(1)}, u32[]{:S(2)}, u32[]{:S(2)}) collective-permute-start(bf16[64,2048]{1,0:T(8,128)(2,1)S(1)} %get-tuple-element.619), channel_id=1, source_target_pairs={{1,0},{2,1},{3,2},{4,3},{5,4},{6,5},{7,6},{8,7},{9,8},{10,9},{11,1... | collective-permute-start | bytes 786440 | tf_op jit(solution)/shard_map/while/body/eval_jaxpr/ppermute | solution.py:14
  356.4 15.5 %collective-permute-start = (bf16[64,2048]{1,0:T(8,128)(2,1)S(1)}, bf16[64,2048]{1,0:T(8,128)(2,1)S(1)}, u32[]{:S(2)}, u32[]{:S(2)}) collective-permute-start(bf16[64,2048]{1,0:T(8,128)(2,1)S(1)} %get-tuple-element.614), channel_id=1, source_target_pairs={{16,0},{17,1},{18,2},{19,3},{20,4},{21,5},{22,6},{23,7},{24,8},{25... | collective-permute-start | bytes 786440 | tf_op jit(solution)/shard_map/while/body/eval_jaxpr/ppermute | solution.py:14
  357.7 20.1 %collective-permute-start.1 = (bf16[64,2048]{1,0:T(8,128)(2,1)S(1)}, bf16[64,2048]{1,0:T(8,128)(2,1)S(1)}, u32[]{:S(2)}, u32[]{:S(2)}) collective-permute-start(bf16[64,2048]{1,0:T(8,128)(2,1)S(1)} %get-tuple-element.615), channel_id=1, source_target_pairs={{8,0},{9,1},{10,2},{11,3},{12,4},{13,5},{14,6},{15,7},{16,8},{17,9... | collective-permute-start | bytes 786440 | tf_op jit(solution)/shard_map/while/body/eval_jaxpr/ppermute | solution.py:14
  359.6 18.2 %collective-permute-start.2 = (bf16[64,2048]{1,0:T(8,128)(2,1)S(1)}, bf16[64,2048]{1,0:T(8,128)(2,1)S(1)}, u32[]{:S(2)}, u32[]{:S(2)}) collective-permute-start(bf16[64,2048]{1,0:T(8,128)(2,1)S(1)} %get-tuple-element.616), channel_id=1, source_target_pairs={{4,0},{5,1},{6,2},{7,3},{8,4},{9,5},{10,6},{11,7},{12,8},{13,9},{1... | collective-permute-start | bytes 786440 | tf_op jit(solution)/shard_map/while/body/eval_jaxpr/ppermute | solution.py:14
  361.5 16.3 %collective-permute-start.3 = (bf16[64,2048]{1,0:T(8,128)(2,1)S(1)}, bf16[64,2048]{1,0:T(8,128)(2,1)S(1)}, u32[]{:S(2)}, u32[]{:S(2)}) collective-permute-start(bf16[64,2048]{1,0:T(8,128)(2,1)S(1)} %get-tuple-element.617), channel_id=1, source_target_pairs={{2,0},{3,1},{4,2},{5,3},{6,4},{7,5},{8,6},{9,7},{10,8},{11,9},{12,... | collective-permute-start | bytes 786440 | tf_op jit(solution)/shard_map/while/body/eval_jaxpr/ppermute | solution.py:14
  364.6 13.7 %collective-permute-start.4 = (bf16[64,2048]{1,0:T(8,128)(2,1)S(1)}, bf16[64,2048]{1,0:T(8,128)(2,1)S(1)}, u32[]{:S(2)}, u32[]{:S(2)}) collective-permute-start(bf16[64,2048]{1,0:T(8,128)(2,1)S(1)} %get-tuple-element.619), channel_id=1, source_target_pairs={{1,0},{2,1},{3,2},{4,3},{5,4},{6,5},{7,6},{8,7},{9,8},{10,9},{11,1... | collective-permute-start | bytes 786440 | tf_op jit(solution)/shard_map/while/body/eval_jaxpr/ppermute | solution.py:14
  380.3 194.2 %collective-permute-start.5 = (bf16[64,1024]{1,0:T(8,128)(2,1)}, bf16[64,1024]{1,0:T(8,128)(2,1)}, u32[]{:S(2)}, u32[]{:S(2)}) collective-permute-start(bf16[64,1024]{1,0:T(8,128)(2,1)} %get-tuple-element.621), channel_id=1, source_target_pairs={{32,0},{64,32},{96,64},{128,96},{160,128},{192,160},{224,192},{33,... | collective-permute-start | bytes 393224 | tf_op jit(solution)/shard_map/while/body/eval_jaxpr/ppermute | solution.py:14
  598.6 15.8 %collective-permute-start = (bf16[64,2048]{1,0:T(8,128)(2,1)S(1)}, bf16[64,2048]{1,0:T(8,128)(2,1)S(1)}, u32[]{:S(2)}, u32[]{:S(2)}) collective-permute-start(bf16[64,2048]{1,0:T(8,128)(2,1)S(1)} %get-tuple-element.614), channel_id=1, source_target_pairs={{16,0},{17,1},{18,2},{19,3},{20,4},{21,5},{22,6},{23,7},{24,8},{25... | collective-permute-start | bytes 786440 | tf_op jit(solution)/shard_map/while/body/eval_jaxpr/ppermute | solution.py:14
  599.9 20.0 %collective-permute-start.1 = (bf16[64,2048]{1,0:T(8,128)(2,1)S(1)}, bf16[64,2048]{1,0:T(8,128)(2,1)S(1)}, u32[]{:S(2)}, u32[]{:S(2)}) collective-permute-start(bf16[64,2048]{1,0:T(8,128)(2,1)S(1)} %get-tuple-element.615), channel_id=1, source_target_pairs={{8,0},{9,1},{10,2},{11,3},{12,4},{13,5},{14,6},{15,7},{16,8},{17,9... | collective-permute-start | bytes 786440 | tf_op jit(solution)/shard_map/while/body/eval_jaxpr/ppermute | solution.py:14
  601.8 18.1 %collective-permute-start.2 = (bf16[64,2048]{1,0:T(8,128)(2,1)S(1)}, bf16[64,2048]{1,0:T(8,128)(2,1)S(1)}, u32[]{:S(2)}, u32[]{:S(2)}) collective-permute-start(bf16[64,2048]{1,0:T(8,128)(2,1)S(1)} %get-tuple-element.616), channel_id=1, source_target_pairs={{4,0},{5,1},{6,2},{7,3},{8,4},{9,5},{10,6},{11,7},{12,8},{13,9},{1... | collective-permute-start | bytes 786440 | tf_op jit(solution)/shard_map/while/body/eval_jaxpr/ppermute | solution.py:14
  603.7 16.2 %collective-permute-start.3 = (bf16[64,2048]{1,0:T(8,128)(2,1)S(1)}, bf16[64,2048]{1,0:T(8,128)(2,1)S(1)}, u32[]{:S(2)}, u32[]{:S(2)}) collective-permute-start(bf16[64,2048]{1,0:T(8,128)(2,1)S(1)} %get-tuple-element.617), channel_id=1, source_target_pairs={{2,0},{3,1},{4,2},{5,3},{6,4},{7,5},{8,6},{9,7},{10,8},{11,9},{12,... | collective-permute-start | bytes 786440 | tf_op jit(solution)/shard_map/while/body/eval_jaxpr/ppermute | solution.py:14
  606.8 14.8 %collective-permute-start.4 = (bf16[64,2048]{1,0:T(8,128)(2,1)S(1)}, bf16[64,2048]{1,0:T(8,128)(2,1)S(1)}, u32[]{:S(2)}, u32[]{:S(2)}) collective-permute-start(bf16[64,2048]{1,0:T(8,128)(2,1)S(1)} %get-tuple-element.619), channel_id=1, source_target_pairs={{1,0},{2,1},{3,2},{4,3},{5,4},{6,5},{7,6},{8,7},{9,8},{10,9},{11,1... | collective-permute-start | bytes 786440 | tf_op jit(solution)/shard_map/while/body/eval_jaxpr/ppermute | solution.py:14
  660.9 18.5 %collective-permute-start = (bf16[64,2048]{1,0:T(8,128)(2,1)S(1)}, bf16[64,2048]{1,0:T(8,128)(2,1)S(1)}, u32[]{:S(2)}, u32[]{:S(2)}) collective-permute-start(bf16[64,2048]{1,0:T(8,128)(2,1)S(1)} %get-tuple-element.614), channel_id=1, source_target_pairs={{16,0},{17,1},{18,2},{19,3},{20,4},{21,5},{22,6},{23,7},{24,8},{25... | collective-permute-start | bytes 786440 | tf_op jit(solution)/shard_map/while/body/eval_jaxpr/ppermute | solution.py:14
  662.2 22.8 %collective-permute-start.1 = (bf16[64,2048]{1,0:T(8,128)(2,1)S(1)}, bf16[64,2048]{1,0:T(8,128)(2,1)S(1)}, u32[]{:S(2)}, u32[]{:S(2)}) collective-permute-start(bf16[64,2048]{1,0:T(8,128)(2,1)S(1)} %get-tuple-element.615), channel_id=1, source_target_pairs={{8,0},{9,1},{10,2},{11,3},{12,4},{13,5},{14,6},{15,7},{16,8},{17,9... | collective-permute-start | bytes 786440 | tf_op jit(solution)/shard_map/while/body/eval_jaxpr/ppermute | solution.py:14
  664.2 20.9 %collective-permute-start.2 = (bf16[64,2048]{1,0:T(8,128)(2,1)S(1)}, bf16[64,2048]{1,0:T(8,128)(2,1)S(1)}, u32[]{:S(2)}, u32[]{:S(2)}) collective-permute-start(bf16[64,2048]{1,0:T(8,128)(2,1)S(1)} %get-tuple-element.616), channel_id=1, source_target_pairs={{4,0},{5,1},{6,2},{7,3},{8,4},{9,5},{10,6},{11,7},{12,8},{13,9},{1... | collective-permute-start | bytes 786440 | tf_op jit(solution)/shard_map/while/body/eval_jaxpr/ppermute | solution.py:14
  666.1 19.0 %collective-permute-start.3 = (bf16[64,2048]{1,0:T(8,128)(2,1)S(1)}, bf16[64,2048]{1,0:T(8,128)(2,1)S(1)}, u32[]{:S(2)}, u32[]{:S(2)}) collective-permute-start(bf16[64,2048]{1,0:T(8,128)(2,1)S(1)} %get-tuple-element.617), channel_id=1, source_target_pairs={{2,0},{3,1},{4,2},{5,3},{6,4},{7,5},{8,6},{9,7},{10,8},{11,9},{12,... | collective-permute-start | bytes 786440 | tf_op jit(solution)/shard_map/while/body/eval_jaxpr/ppermute | solution.py:14
  669.2 15.9 %collective-permute-start.4 = (bf16[64,2048]{1,0:T(8,128)(2,1)S(1)}, bf16[64,2048]{1,0:T(8,128)(2,1)S(1)}, u32[]{:S(2)}, u32[]{:S(2)}) collective-permute-start(bf16[64,2048]{1,0:T(8,128)(2,1)S(1)} %get-tuple-element.619), channel_id=1, source_target_pairs={{1,0},{2,1},{3,2},{4,3},{5,4},{6,5},{7,6},{8,7},{9,8},{10,9},{11,1... | collective-permute-start | bytes 786440 | tf_op jit(solution)/shard_map/while/body/eval_jaxpr/ppermute | solution.py:14
  (45 other events, 416.6 us)
Sparse Core Ops, SparseCore 0:
  14.5 80.5 all-gather.1
  715.3 107.4 reduce-scatter.1
where the time goes:
time: 836 us; the launch traced here: 832 us
  waiting for transfers between devices  514 us (61%)
  starting transfers between devices  110 us (13%)
  local copies, waits for them, and re-layouts  74.5 us (9%)
  other arithmetic  72.8 us (9%)
  matrix products  44.7 us (5%)
  between operations  14.3 us (2%)
    ppermute x54, waiting for transfers between devices, shifted(): lax.ppermute(value, axis, [(source, source + steps) for source in range(i...  328 us
    ppermute x54, starting transfers between devices, shifted(): lax.ppermute(value, axis, [(source, source + steps) for source in range(i...  110 us
    reduce_scatter x1, waiting for transfers between devices, per_device(): lax.psum_scatter(jnp.concatenate([first, second], 1).astype(jnp.bfloat16)...  108 us
    all_gather x1, waiting for transfers between devices, per_device(): every_pair = lax.all_gather(pairs, 'tm', axis=1, tiled=True)  78.4 us
    select_n x9, other arithmetic, step(): jnp.where(active, lax.dynamic_update_index_in_dim(qkv_store, qkv_grad, sl...  16.7 us
  transfers between devices with their start and end apart: 56, of which 42 were waited for; matrix products, arithmetic and copies ran while one was open for 4% of the time, Pallas kernels for 0%

commit v1 on v0

--- a/solution.py
+++ b/solution.py
@@ -107,7 +107,9 @@
     qkv = jnp.dot(rounded_norm.reshape(-1, model_width), w_qkv, preferred_element_type=jnp.float32)
     qkv = qkv.astype(jnp.bfloat16).reshape(micro_count, shard_rows, 3 * model_width)
     pairs = qkv[..., model_width:]
-    every_pair = lax.all_gather(pairs, "tm", axis=1, tiled=True)
+    every_pair = jnp.concatenate(
+        lax.all_to_all(jnp.stack([pairs] * lax.axis_size("tm")), "tm", 0, 0), axis=1
+    )
     shard_index = lax.axis_index("tm")
     far_list = []
     for level in range(levels):

time: 836 us -> 1040 us (1.24)
  waiting for transfers between devices: 514 us -> 659 us
  starting transfers between devices: 110 us -> 163 us
    all_to_all x0 -> x1, waiting for transfers between devices: none -> 222 us  [per_device(): lax.all_to_all(jnp.stack([pairs] * lax.axis_size('tm')), 'tm', 0, 0)]
    all_gather x1 -> x0, waiting for transfers between devices: 78.4 us -> none  [per_device(): every_pair = lax.all_gather(pairs, 'tm', axis=1, tiled=True)]
    ppermute x54, starting transfers between devices: 110 us -> 155 us  [shifted(): lax.ppermute(value, axis, [(source, source + steps) for source in range(i...]
  transfers between devices with their start and end apart: 56 -> 56, of which waited for: 42 -> 41; matrix products, arithmetic and copies ran while one was open for 4% -> 3% of each run, Pallas kernels for 0% -> 0%
where the time goes in v1:
time: 1040 us
  waiting for transfers between devices  659 us (63%)
  starting transfers between devices  163 us (16%)
  local copies, waits for them, and re-layouts  81 us (8%)
  other arithmetic  72.4 us (7%)
  matrix products  43.9 us (4%)
  between operations  14.3 us (1%)
    ppermute x54, waiting for transfers between devices, shifted(): lax.ppermute(value, axis, [(source, source + steps) for source in range(i...  328 us
    all_to_all x1, waiting for transfers between devices, per_device(): lax.all_to_all(jnp.stack([pairs] * lax.axis_size('tm')), 'tm', 0, 0)  222 us
    ppermute x54, starting transfers between devices, shifted(): lax.ppermute(value, axis, [(source, source + steps) for source in range(i...  155 us
    reduce_scatter x1, waiting for transfers between devices, per_device(): lax.psum_scatter(jnp.concatenate([first, second], 1).astype(jnp.bfloat16)...  109 us
  transfers between devices with their start and end apart: 56, of which 41 were waited for; matrix products, arithmetic and copies ran while one was open for 3% of the time, Pallas kernels for 0%

profile of v1, /device:TPU:2, one launch (start us, length us, event | category | flops | bytes accessed | tf_op | source)
XLA Modules:
  0.0 1035.7 jit_solution(6617794576744270416)
XLA Ops:
  9.3 3.8 convolution_convert_fusion.1
  14.1 6.0 stack.4
  20.1 7.8 all-to-all-start
  30.4 222.0 %all-to-all-done = bf16[32,2,64,2048]{3,2,1,0:T(8,128)(2,1)} async-done(((bf16[32,2,64,2048]{3,2,1,0:T(8,128)(2,1)}), bf16[32,2,64,2048]{3,2,1,0:T(8,128)(2,1)}, u32[]{:S(2)}, u32[]{:S(2)}) %all-to-all-start) | async-done | bytes 16777248 | tf_op jit(solution)/shard_map/all_to_all | solution.py:111
  252.4 8.1 copy.77
  269.1 3.1 fusion.51
  282.7 620.6 %while.21 = (s32[]{:T(128)}, bf16[64,1024]{1,0:T(8,128)(2,1)}, bf16[2,64,1024]{2,1,0:T(8,128)(2,1)}, bf16[2,64,3072]{2,1,0:T(8,128)(2,1)}, bf16[2,64,1024]{2,1,0...) while((s32[]{:T(128)}, bf16[64,1024]{1,0:T(8,128)(2,1)}, ...), condition=%wide.region_13.14_spmd, body=%wide.region_5.13_spmd.sunk | while | flops 800390528 | bytes 102196128 | solution.py:198
  287.8 18.0 %collective-permute-start.1 = (bf16[64,2048]{1,0:T(8,128)(2,1)S(1)}, bf16[64,2048]{1,0:T(8,128)(2,1)S(1)}, u32[]{:S(2)}, u32[]{:S(2)}) collective-permute-start(bf16[64,2048]{1,0:T(8,128)(2,1)S(1)} %get-tuple-element.647), channel_id=1, source_target_pairs={{8,0},{9,1},{10,2},{11,3},{12,4},{13,5},{14,6},{15,7},{16,8},{17,9... | collective-permute-start | bytes 786440 | tf_op jit(solution)/shard_map/while/body/eval_jaxpr/ppermute | solution.py:14
  307.7 32.9 %collective-permute-start.3 = (bf16[64,2048]{1,0:T(8,128)(2,1)S(1)}, bf16[64,2048]{1,0:T(8,128)(2,1)S(1)}, u32[]{:S(2)}, u32[]{:S(2)}) collective-permute-start(bf16[64,2048]{1,0:T(8,128)(2,1)S(1)} %get-tuple-element.649), channel_id=1, source_target_pairs={{2,0},{3,1},{4,2},{5,3},{6,4},{7,5},{8,6},{9,7},{10,8},{11,9},{12,... | collective-permute-start | bytes 786440 | tf_op jit(solution)/shard_map/while/body/eval_jaxpr/ppermute | solution.py:14
  342.6 7.8 collective-permute-done.3
  374.6 3.2 collective-permute-start.4
  379.3 3.9 collective-permute-done.1
  383.2 3.8 collective-permute-done.3
  396.6 3.2 collective-permute-done.5
  411.1 3.2 collective-permute-start.4
  414.3 4.6 collective-permute-done
  418.8 3.8 collective-permute-done.1
  434.1 3.8 collective-permute-done.5
  453.6 5.6 collective-permute-done.1
  471.7 4.6 collective-permute-done.5
  487.2 3.2 collective-permute-start.4
  492.4 5.8 collective-permute-done.1
  510.1 4.9 collective-permute-done.5
  525.9 3.2 collective-permute-start.4
  529.1 3.0 collective-permute-done
  532.1 5.6 collective-permute-done.1
  548.8 3.6 collective-permute-done.5
  563.9 3.3 collective-permute-start.4
  567.2 4.2 collective-permute-done
  571.3 5.6 collective-permute-done.1
  585.7 189.8 %collective-permute-done.5 = bf16[64,1024]{1,0:T(8,128)(2,1)} collective-permute-done((bf16[64,1024]{1,0:T(8,128)(2,1)}, bf16[64,1024]{1,0:T(8,128)(2,1)}, u32[]{:S(2)}, u32[]{:S(2)}) %collective-permute-start.5) | collective-permute-done | bytes 131104 | tf_op jit(solution)/shard_map/while/body/eval_jaxpr/ppermute | solution.py:14
  777.2 22.2 %conditional.4 = (bf16[5,64,2048]{2,1,0:T(8,128)(2,1)S(1)}, f32[64,2048]{1,0:T(8,128)}, bf16[64,1024]{1,0:T(8,128)(2,1)S(1)}, bf16[1,64,1024]{2,1,0:T(8,128)(2,1)S(1)}) conditional(s32[]{:T(128)} %convert_element_type.218, () %tuple.95, (s32[]{:T(128)}, bf16[2,384,2048]{1,2,0:T(8,128)(2,1)}, pred[64,384]{1,0:T(8,128)(4,1)S(1)}, ...), branch_computations={%region_6.6_spmd, %region_7.9_spmd} | conditional | flops 393805184 | bytes 68178248 | solution.py:171
  805.5 3.1 collective-permute-start.3
  808.6 3.3 collective-permute-start.4
  811.9 4.3 collective-permute-done
  816.2 5.3 collective-permute-done.1
  824.8 6.8 conditional.5
  824.8 5.1 fusion
  840.6 22.2 %conditional.4 = (bf16[5,64,2048]{2,1,0:T(8,128)(2,1)S(1)}, f32[64,2048]{1,0:T(8,128)}, bf16[64,1024]{1,0:T(8,128)(2,1)S(1)}, bf16[1,64,1024]{2,1,0:T(8,128)(2,1)S(1)}) conditional(s32[]{:T(128)} %convert_element_type.218, () %tuple.95, (s32[]{:T(128)}, bf16[2,384,2048]{1,2,0:T(8,128)(2,1)}, pred[64,384]{1,0:T(8,128)(4,1)S(1)}, ...), branch_computations={%region_6.6_spmd, %region_7.9_spmd} | conditional | flops 393805184 | bytes 68178248 | solution.py:171
  869.0 3.1 collective-permute-start.3
  872.1 3.2 collective-permute-start.4
  875.3 6.7 collective-permute-done
  882.0 5.8 collective-permute-done.1
  889.1 6.8 conditional.5
  889.1 5.1 fusion
  903.4 5.9 bitcast_convert_fusion
  910.9 6.9 pad_maximum_fusion.3
  917.8 108.6 %reduce-scatter.2.cloned.1.call-done = bf16[32,4096]{1,0:T(8,128)(2,1)} async-done(((bf16[1024,4096]{1,0:T(8,128)(2,1)}), bf16[32,4096]{1,0:T(8,128)(2,1)}) %reduce-scatter.2.cloned.1.call-update) | async-done | bytes 262160 | tf_op jit(solution)/shard_map/reduce_scatter | solution.py:210
  (476 shorter events, 283.8 us)
Async XLA Ops:
  20.1 232.2 %all-to-all-start = ((bf16[32,2,64,2048]{3,2,1,0:T(8,128)(2,1)}), bf16[32,2,64,2048]{3,2,1,0:T(8,128)(2,1)}, u32[]{:S(2)}, u32[]{:S(2)}) async-start(bf16[32,2,64,2048]{3,2,1,0:T(8,128)(2,1)} %stack.4), calls=%async_computation | async-start | bytes 33554432 | tf_op jit(solution)/shard_map/all_to_all | solution.py:111
  28.0 998.4 %reduce-scatter.2.cloned.1.call-start = ((), (), s32[]{:S(2)}) async-start(), calls=%async_computation.2 | async-start | bytes 8650752 | tf_op jit(solution)/shard_map/reduce_scatter | solution.py:210
  286.4 56.2 %collective-permute-start = (bf16[64,2048]{1,0:T(8,128)(2,1)S(1)}, bf16[64,2048]{1,0:T(8,128)(2,1)S(1)}, u32[]{:S(2)}, u32[]{:S(2)}) collective-permute-start(bf16[64,2048]{1,0:T(8,128)(2,1)S(1)} %get-tuple-element.646), channel_id=1, source_target_pairs={{16,0},{17,1},{18,2},{19,3},{20,4},{21,5},{22,6},{23,7},{24,8},{25... | collective-permute-start | bytes 786440 | tf_op jit(solution)/shard_map/while/body/eval_jaxpr/ppermute | solution.py:14
  287.8 54.8 %collective-permute-start.1 = (bf16[64,2048]{1,0:T(8,128)(2,1)S(1)}, bf16[64,2048]{1,0:T(8,128)(2,1)S(1)}, u32[]{:S(2)}, u32[]{:S(2)}) collective-permute-start(bf16[64,2048]{1,0:T(8,128)(2,1)S(1)} %get-tuple-element.647), channel_id=1, source_target_pairs={{8,0},{9,1},{10,2},{11,3},{12,4},{13,5},{14,6},{15,7},{16,8},{17,9... | collective-permute-start | bytes 786440 | tf_op jit(solution)/shard_map/while/body/eval_jaxpr/ppermute | solution.py:14
  305.8 36.8 %collective-permute-start.2 = (bf16[64,2048]{1,0:T(8,128)(2,1)S(1)}, bf16[64,2048]{1,0:T(8,128)(2,1)S(1)}, u32[]{:S(2)}, u32[]{:S(2)}) collective-permute-start(bf16[64,2048]{1,0:T(8,128)(2,1)S(1)} %get-tuple-element.648), channel_id=1, source_target_pairs={{4,0},{5,1},{6,2},{7,3},{8,4},{9,5},{10,6},{11,7},{12,8},{13,9},{1... | collective-permute-start | bytes 786440 | tf_op jit(solution)/shard_map/while/body/eval_jaxpr/ppermute | solution.py:14
  307.7 42.7 %collective-permute-start.3 = (bf16[64,2048]{1,0:T(8,128)(2,1)S(1)}, bf16[64,2048]{1,0:T(8,128)(2,1)S(1)}, u32[]{:S(2)}, u32[]{:S(2)}) collective-permute-start(bf16[64,2048]{1,0:T(8,128)(2,1)S(1)} %get-tuple-element.649), channel_id=1, source_target_pairs={{2,0},{3,1},{4,2},{5,3},{6,4},{7,5},{8,6},{9,7},{10,8},{11,9},{12,... | collective-permute-start | bytes 786440 | tf_op jit(solution)/shard_map/while/body/eval_jaxpr/ppermute | solution.py:14
  340.7 12.6 %collective-permute-start.4 = (bf16[64,2048]{1,0:T(8,128)(2,1)S(1)}, bf16[64,2048]{1,0:T(8,128)(2,1)S(1)}, u32[]{:S(2)}, u32[]{:S(2)}) collective-permute-start(bf16[64,2048]{1,0:T(8,128)(2,1)S(1)} %get-tuple-element.651), channel_id=1, source_target_pairs={{1,0},{2,1},{3,2},{4,3},{5,4},{6,5},{7,6},{8,7},{9,8},{10,9},{11,1... | collective-permute-start | bytes 786440 | tf_op jit(solution)/shard_map/while/body/eval_jaxpr/ppermute | solution.py:14
  366.6 12.7 %collective-permute-start = (bf16[64,2048]{1,0:T(8,128)(2,1)S(1)}, bf16[64,2048]{1,0:T(8,128)(2,1)S(1)}, u32[]{:S(2)}, u32[]{:S(2)}) collective-permute-start(bf16[64,2048]{1,0:T(8,128)(2,1)S(1)} %get-tuple-element.646), channel_id=1, source_target_pairs={{16,0},{17,1},{18,2},{19,3},{20,4},{21,5},{22,6},{23,7},{24,8},{25... | collective-permute-start | bytes 786440 | tf_op jit(solution)/shard_map/while/body/eval_jaxpr/ppermute | solution.py:14
  368.0 15.2 %collective-permute-start.1 = (bf16[64,2048]{1,0:T(8,128)(2,1)S(1)}, bf16[64,2048]{1,0:T(8,128)(2,1)S(1)}, u32[]{:S(2)}, u32[]{:S(2)}) collective-permute-start(bf16[64,2048]{1,0:T(8,128)(2,1)S(1)} %get-tuple-element.647), channel_id=1, source_target_pairs={{8,0},{9,1},{10,2},{11,3},{12,4},{13,5},{14,6},{15,7},{16,8},{17,9... | collective-permute-start | bytes 786440 | tf_op jit(solution)/shard_map/while/body/eval_jaxpr/ppermute | solution.py:14
  370.0 13.3 %collective-permute-start.2 = (bf16[64,2048]{1,0:T(8,128)(2,1)S(1)}, bf16[64,2048]{1,0:T(8,128)(2,1)S(1)}, u32[]{:S(2)}, u32[]{:S(2)}) collective-permute-start(bf16[64,2048]{1,0:T(8,128)(2,1)S(1)} %get-tuple-element.648), channel_id=1, source_target_pairs={{4,0},{5,1},{6,2},{7,3},{8,4},{9,5},{10,6},{11,7},{12,8},{13,9},{1... | collective-permute-start | bytes 786440 | tf_op jit(solution)/shard_map/while/body/eval_jaxpr/ppermute | solution.py:14
  371.9 15.1 %collective-permute-start.3 = (bf16[64,2048]{1,0:T(8,128)(2,1)S(1)}, bf16[64,2048]{1,0:T(8,128)(2,1)S(1)}, u32[]{:S(2)}, u32[]{:S(2)}) collective-permute-start(bf16[64,2048]{1,0:T(8,128)(2,1)S(1)} %get-tuple-element.649), channel_id=1, source_target_pairs={{2,0},{3,1},{4,2},{5,3},{6,4},{7,5},{8,6},{9,7},{10,8},{11,9},{12,... | collective-permute-start | bytes 786440 | tf_op jit(solution)/shard_map/while/body/eval_jaxpr/ppermute | solution.py:14
  374.6 15.3 %collective-permute-start.4 = (bf16[64,2048]{1,0:T(8,128)(2,1)S(1)}, bf16[64,2048]{1,0:T(8,128)(2,1)S(1)}, u32[]{:S(2)}, u32[]{:S(2)}) collective-permute-start(bf16[64,2048]{1,0:T(8,128)(2,1)S(1)} %get-tuple-element.651), channel_id=1, source_target_pairs={{1,0},{2,1},{3,2},{4,3},{5,4},{6,5},{7,6},{8,7},{9,8},{10,9},{11,1... | collective-permute-start | bytes 786440 | tf_op jit(solution)/shard_map/while/body/eval_jaxpr/ppermute | solution.py:14
  403.4 15.4 %collective-permute-start = (bf16[64,2048]{1,0:T(8,128)(2,1)S(1)}, bf16[64,2048]{1,0:T(8,128)(2,1)S(1)}, u32[]{:S(2)}, u32[]{:S(2)}) collective-permute-start(bf16[64,2048]{1,0:T(8,128)(2,1)S(1)} %get-tuple-element.646), channel_id=1, source_target_pairs={{16,0},{17,1},{18,2},{19,3},{20,4},{21,5},{22,6},{23,7},{24,8},{25... | collective-permute-start | bytes 786440 | tf_op jit(solution)/shard_map/while/body/eval_jaxpr/ppermute | solution.py:14
  404.9 17.7 %collective-permute-start.1 = (bf16[64,2048]{1,0:T(8,128)(2,1)S(1)}, bf16[64,2048]{1,0:T(8,128)(2,1)S(1)}, u32[]{:S(2)}, u32[]{:S(2)}) collective-permute-start(bf16[64,2048]{1,0:T(8,128)(2,1)S(1)} %get-tuple-element.647), channel_id=1, source_target_pairs={{8,0},{9,1},{10,2},{11,3},{12,4},{13,5},{14,6},{15,7},{16,8},{17,9... | collective-permute-start | bytes 786440 | tf_op jit(solution)/shard_map/while/body/eval_jaxpr/ppermute | solution.py:14
  406.8 15.8 %collective-permute-start.2 = (bf16[64,2048]{1,0:T(8,128)(2,1)S(1)}, bf16[64,2048]{1,0:T(8,128)(2,1)S(1)}, u32[]{:S(2)}, u32[]{:S(2)}) collective-permute-start(bf16[64,2048]{1,0:T(8,128)(2,1)S(1)} %get-tuple-element.648), channel_id=1, source_target_pairs={{4,0},{5,1},{6,2},{7,3},{8,4},{9,5},{10,6},{11,7},{12,8},{13,9},{1... | collective-permute-start | bytes 786440 | tf_op jit(solution)/shard_map/while/body/eval_jaxpr/ppermute | solution.py:14
  408.7 16.6 %collective-permute-start.3 = (bf16[64,2048]{1,0:T(8,128)(2,1)S(1)}, bf16[64,2048]{1,0:T(8,128)(2,1)S(1)}, u32[]{:S(2)}, u32[]{:S(2)}) collective-permute-start(bf16[64,2048]{1,0:T(8,128)(2,1)S(1)} %get-tuple-element.649), channel_id=1, source_target_pairs={{2,0},{3,1},{4,2},{5,3},{6,4},{7,5},{8,6},{9,7},{10,8},{11,9},{12,... | collective-permute-start | bytes 786440 | tf_op jit(solution)/shard_map/while/body/eval_jaxpr/ppermute | solution.py:14
  411.1 16.2 %collective-permute-start.4 = (bf16[64,2048]{1,0:T(8,128)(2,1)S(1)}, bf16[64,2048]{1,0:T(8,128)(2,1)S(1)}, u32[]{:S(2)}, u32[]{:S(2)}) collective-permute-start(bf16[64,2048]{1,0:T(8,128)(2,1)S(1)} %get-tuple-element.651), channel_id=1, source_target_pairs={{1,0},{2,1},{3,2},{4,3},{5,4},{6,5},{7,6},{8,7},{9,8},{10,9},{11,1... | collective-permute-start | bytes 786440 | tf_op jit(solution)/shard_map/while/body/eval_jaxpr/ppermute | solution.py:14
  441.5 12.2 %collective-permute-start = (bf16[64,2048]{1,0:T(8,128)(2,1)S(1)}, bf16[64,2048]{1,0:T(8,128)(2,1)S(1)}, u32[]{:S(2)}, u32[]{:S(2)}) collective-permute-start(bf16[64,2048]{1,0:T(8,128)(2,1)S(1)} %get-tuple-element.646), channel_id=1, source_target_pairs={{16,0},{17,1},{18,2},{19,3},{20,4},{21,5},{22,6},{23,7},{24,8},{25... | collective-permute-start | bytes 786440 | tf_op jit(solution)/shard_map/while/body/eval_jaxpr/ppermute | solution.py:14
  442.9 16.3 %collective-permute-start.1 = (bf16[64,2048]{1,0:T(8,128)(2,1)S(1)}, bf16[64,2048]{1,0:T(8,128)(2,1)S(1)}, u32[]{:S(2)}, u32[]{:S(2)}) collective-permute-start(bf16[64,2048]{1,0:T(8,128)(2,1)S(1)} %get-tuple-element.647), channel_id=1, source_target_pairs={{8,0},{9,1},{10,2},{11,3},{12,4},{13,5},{14,6},{15,7},{16,8},{17,9... | collective-permute-start | bytes 786440 | tf_op jit(solution)/shard_map/while/body/eval_jaxpr/ppermute | solution.py:14
  444.8 14.4 %collective-permute-start.2 = (bf16[64,2048]{1,0:T(8,128)(2,1)S(1)}, bf16[64,2048]{1,0:T(8,128)(2,1)S(1)}, u32[]{:S(2)}, u32[]{:S(2)}) collective-permute-start(bf16[64,2048]{1,0:T(8,128)(2,1)S(1)} %get-tuple-element.648), channel_id=1, source_target_pairs={{4,0},{5,1},{6,2},{7,3},{8,4},{9,5},{10,6},{11,7},{12,8},{13,9},{1... | collective-permute-start | bytes 786440 | tf_op jit(solution)/shard_map/while/body/eval_jaxpr/ppermute | solution.py:14
  446.8 15.4 %collective-permute-start.3 = (bf16[64,2048]{1,0:T(8,128)(2,1)S(1)}, bf16[64,2048]{1,0:T(8,128)(2,1)S(1)}, u32[]{:S(2)}, u32[]{:S(2)}) collective-permute-start(bf16[64,2048]{1,0:T(8,128)(2,1)S(1)} %get-tuple-element.649), channel_id=1, source_target_pairs={{2,0},{3,1},{4,2},{5,3},{6,4},{7,5},{8,6},{9,7},{10,8},{11,9},{12,... | collective-permute-start | bytes 786440 | tf_op jit(solution)/shard_map/while/body/eval_jaxpr/ppermute | solution.py:14
  448.7 16.2 %collective-permute-start.4 = (bf16[64,2048]{1,0:T(8,128)(2,1)S(1)}, bf16[64,2048]{1,0:T(8,128)(2,1)S(1)}, u32[]{:S(2)}, u32[]{:S(2)}) collective-permute-start(bf16[64,2048]{1,0:T(8,128)(2,1)S(1)} %get-tuple-element.651), channel_id=1, source_target_pairs={{1,0},{2,1},{3,2},{4,3},{5,4},{6,5},{7,6},{8,7},{9,8},{10,9},{11,1... | collective-permute-start | bytes 786440 | tf_op jit(solution)/shard_map/while/body/eval_jaxpr/ppermute | solution.py:14
  480.0 12.4 %collective-permute-start = (bf16[64,2048]{1,0:T(8,128)(2,1)S(1)}, bf16[64,2048]{1,0:T(8,128)(2,1)S(1)}, u32[]{:S(2)}, u32[]{:S(2)}) collective-permute-start(bf16[64,2048]{1,0:T(8,128)(2,1)S(1)} %get-tuple-element.646), channel_id=1, source_target_pairs={{16,0},{17,1},{18,2},{19,3},{20,4},{21,5},{22,6},{23,7},{24,8},{25... | collective-permute-start | bytes 786440 | tf_op jit(solution)/shard_map/while/body/eval_jaxpr/ppermute | solution.py:14
  481.4 16.7 %collective-permute-start.1 = (bf16[64,2048]{1,0:T(8,128)(2,1)S(1)}, bf16[64,2048]{1,0:T(8,128)(2,1)S(1)}, u32[]{:S(2)}, u32[]{:S(2)}) collective-permute-start(bf16[64,2048]{1,0:T(8,128)(2,1)S(1)} %get-tuple-element.647), channel_id=1, source_target_pairs={{8,0},{9,1},{10,2},{11,3},{12,4},{13,5},{14,6},{15,7},{16,8},{17,9... | collective-permute-start | bytes 786440 | tf_op jit(solution)/shard_map/while/body/eval_jaxpr/ppermute | solution.py:14
  483.4 14.8 %collective-permute-start.2 = (bf16[64,2048]{1,0:T(8,128)(2,1)S(1)}, bf16[64,2048]{1,0:T(8,128)(2,1)S(1)}, u32[]{:S(2)}, u32[]{:S(2)}) collective-permute-start(bf16[64,2048]{1,0:T(8,128)(2,1)S(1)} %get-tuple-element.648), channel_id=1, source_target_pairs={{4,0},{5,1},{6,2},{7,3},{8,4},{9,5},{10,6},{11,7},{12,8},{13,9},{1... | collective-permute-start | bytes 786440 | tf_op jit(solution)/shard_map/while/body/eval_jaxpr/ppermute | solution.py:14
  485.3 15.2 %collective-permute-start.3 = (bf16[64,2048]{1,0:T(8,128)(2,1)S(1)}, bf16[64,2048]{1,0:T(8,128)(2,1)S(1)}, u32[]{:S(2)}, u32[]{:S(2)}) collective-permute-start(bf16[64,2048]{1,0:T(8,128)(2,1)S(1)} %get-tuple-element.649), channel_id=1, source_target_pairs={{2,0},{3,1},{4,2},{5,3},{6,4},{7,5},{8,6},{9,7},{10,8},{11,9},{12,... | collective-permute-start | bytes 786440 | tf_op jit(solution)/shard_map/while/body/eval_jaxpr/ppermute | solution.py:14
  487.2 16.1 %collective-permute-start.4 = (bf16[64,2048]{1,0:T(8,128)(2,1)S(1)}, bf16[64,2048]{1,0:T(8,128)(2,1)S(1)}, u32[]{:S(2)}, u32[]{:S(2)}) collective-permute-start(bf16[64,2048]{1,0:T(8,128)(2,1)S(1)} %get-tuple-element.651), channel_id=1, source_target_pairs={{1,0},{2,1},{3,2},{4,3},{5,4},{6,5},{7,6},{8,7},{9,8},{10,9},{11,1... | collective-permute-start | bytes 786440 | tf_op jit(solution)/shard_map/while/body/eval_jaxpr/ppermute | solution.py:14
  518.7 13.4 %collective-permute-start = (bf16[64,2048]{1,0:T(8,128)(2,1)S(1)}, bf16[64,2048]{1,0:T(8,128)(2,1)S(1)}, u32[]{:S(2)}, u32[]{:S(2)}) collective-permute-start(bf16[64,2048]{1,0:T(8,128)(2,1)S(1)} %get-tuple-element.646), channel_id=1, source_target_pairs={{16,0},{17,1},{18,2},{19,3},{20,4},{21,5},{22,6},{23,7},{24,8},{25... | collective-permute-start | bytes 786440 | tf_op jit(solution)/shard_map/while/body/eval_jaxpr/ppermute | solution.py:14
  520.1 17.5 %collective-permute-start.1 = (bf16[64,2048]{1,0:T(8,128)(2,1)S(1)}, bf16[64,2048]{1,0:T(8,128)(2,1)S(1)}, u32[]{:S(2)}, u32[]{:S(2)}) collective-permute-start(bf16[64,2048]{1,0:T(8,128)(2,1)S(1)} %get-tuple-element.647), channel_id=1, source_target_pairs={{8,0},{9,1},{10,2},{11,3},{12,4},{13,5},{14,6},{15,7},{16,8},{17,9... | collective-permute-start | bytes 786440 | tf_op jit(solution)/shard_map/while/body/eval_jaxpr/ppermute | solution.py:14
  522.1 15.6 %collective-permute-start.2 = (bf16[64,2048]{1,0:T(8,128)(2,1)S(1)}, bf16[64,2048]{1,0:T(8,128)(2,1)S(1)}, u32[]{:S(2)}, u32[]{:S(2)}) collective-permute-start(bf16[64,2048]{1,0:T(8,128)(2,1)S(1)} %get-tuple-element.648), channel_id=1, source_target_pairs={{4,0},{5,1},{6,2},{7,3},{8,4},{9,5},{10,6},{11,7},{12,8},{13,9},{1... | collective-permute-start | bytes 786440 | tf_op jit(solution)/shard_map/while/body/eval_jaxpr/ppermute | solution.py:14
  524.0 15.3 %collective-permute-start.3 = (bf16[64,2048]{1,0:T(8,128)(2,1)S(1)}, bf16[64,2048]{1,0:T(8,128)(2,1)S(1)}, u32[]{:S(2)}, u32[]{:S(2)}) collective-permute-start(bf16[64,2048]{1,0:T(8,128)(2,1)S(1)} %get-tuple-element.649), channel_id=1, source_target_pairs={{2,0},{3,1},{4,2},{5,3},{6,4},{7,5},{8,6},{9,7},{10,8},{11,9},{12,... | collective-permute-start | bytes 786440 | tf_op jit(solution)/shard_map/while/body/eval_jaxpr/ppermute | solution.py:14
  525.9 16.2 %collective-permute-start.4 = (bf16[64,2048]{1,0:T(8,128)(2,1)S(1)}, bf16[64,2048]{1,0:T(8,128)(2,1)S(1)}, u32[]{:S(2)}, u32[]{:S(2)}) collective-permute-start(bf16[64,2048]{1,0:T(8,128)(2,1)S(1)} %get-tuple-element.651), channel_id=1, source_target_pairs={{1,0},{2,1},{3,2},{4,3},{5,4},{6,5},{7,6},{8,7},{9,8},{10,9},{11,1... | collective-permute-start | bytes 786440 | tf_op jit(solution)/shard_map/while/body/eval_jaxpr/ppermute | solution.py:14
  556.1 15.3 %collective-permute-start = (bf16[64,2048]{1,0:T(8,128)(2,1)S(1)}, bf16[64,2048]{1,0:T(8,128)(2,1)S(1)}, u32[]{:S(2)}, u32[]{:S(2)}) collective-permute-start(bf16[64,2048]{1,0:T(8,128)(2,1)S(1)} %get-tuple-element.646), channel_id=1, source_target_pairs={{16,0},{17,1},{18,2},{19,3},{20,4},{21,5},{22,6},{23,7},{24,8},{25... | collective-permute-start | bytes 786440 | tf_op jit(solution)/shard_map/while/body/eval_jaxpr/ppermute | solution.py:14
  557.5 19.4 %collective-permute-start.1 = (bf16[64,2048]{1,0:T(8,128)(2,1)S(1)}, bf16[64,2048]{1,0:T(8,128)(2,1)S(1)}, u32[]{:S(2)}, u32[]{:S(2)}) collective-permute-start(bf16[64,2048]{1,0:T(8,128)(2,1)S(1)} %get-tuple-element.647), channel_id=1, source_target_pairs={{8,0},{9,1},{10,2},{11,3},{12,4},{13,5},{14,6},{15,7},{16,8},{17,9... | collective-permute-start | bytes 786440 | tf_op jit(solution)/shard_map/while/body/eval_jaxpr/ppermute | solution.py:14
  559.5 17.5 %collective-permute-start.2 = (bf16[64,2048]{1,0:T(8,128)(2,1)S(1)}, bf16[64,2048]{1,0:T(8,128)(2,1)S(1)}, u32[]{:S(2)}, u32[]{:S(2)}) collective-permute-start(bf16[64,2048]{1,0:T(8,128)(2,1)S(1)} %get-tuple-element.648), channel_id=1, source_target_pairs={{4,0},{5,1},{6,2},{7,3},{8,4},{9,5},{10,6},{11,7},{12,8},{13,9},{1... | collective-permute-start | bytes 786440 | tf_op jit(solution)/shard_map/while/body/eval_jaxpr/ppermute | solution.py:14
  561.4 15.5 %collective-permute-start.3 = (bf16[64,2048]{1,0:T(8,128)(2,1)S(1)}, bf16[64,2048]{1,0:T(8,128)(2,1)S(1)}, u32[]{:S(2)}, u32[]{:S(2)}) collective-permute-start(bf16[64,2048]{1,0:T(8,128)(2,1)S(1)} %get-tuple-element.649), channel_id=1, source_target_pairs={{2,0},{3,1},{4,2},{5,3},{6,4},{7,5},{8,6},{9,7},{10,8},{11,9},{12,... | collective-permute-start | bytes 786440 | tf_op jit(solution)/shard_map/while/body/eval_jaxpr/ppermute | solution.py:14
  563.9 15.0 %collective-permute-start.4 = (bf16[64,2048]{1,0:T(8,128)(2,1)S(1)}, bf16[64,2048]{1,0:T(8,128)(2,1)S(1)}, u32[]{:S(2)}, u32[]{:S(2)}) collective-permute-start(bf16[64,2048]{1,0:T(8,128)(2,1)S(1)} %get-tuple-element.651), channel_id=1, source_target_pairs={{1,0},{2,1},{3,2},{4,3},{5,4},{6,5},{7,6},{8,7},{9,8},{10,9},{11,1... | collective-permute-start | bytes 786440 | tf_op jit(solution)/shard_map/while/body/eval_jaxpr/ppermute | solution.py:14
  580.9 194.5 %collective-permute-start.5 = (bf16[64,1024]{1,0:T(8,128)(2,1)}, bf16[64,1024]{1,0:T(8,128)(2,1)}, u32[]{:S(2)}, u32[]{:S(2)}) collective-permute-start(bf16[64,1024]{1,0:T(8,128)(2,1)} %get-tuple-element.653), channel_id=1, source_target_pairs={{32,0},{64,32},{96,64},{128,96},{160,128},{192,160},{224,192},{33,... | collective-permute-start | bytes 393224 | tf_op jit(solution)/shard_map/while/body/eval_jaxpr/ppermute | solution.py:14
  800.2 16.0 %collective-permute-start = (bf16[64,2048]{1,0:T(8,128)(2,1)S(1)}, bf16[64,2048]{1,0:T(8,128)(2,1)S(1)}, u32[]{:S(2)}, u32[]{:S(2)}) collective-permute-start(bf16[64,2048]{1,0:T(8,128)(2,1)S(1)} %get-tuple-element.646), channel_id=1, source_target_pairs={{16,0},{17,1},{18,2},{19,3},{20,4},{21,5},{22,6},{23,7},{24,8},{25... | collective-permute-start | bytes 786440 | tf_op jit(solution)/shard_map/while/body/eval_jaxpr/ppermute | solution.py:14
  801.7 19.9 %collective-permute-start.1 = (bf16[64,2048]{1,0:T(8,128)(2,1)S(1)}, bf16[64,2048]{1,0:T(8,128)(2,1)S(1)}, u32[]{:S(2)}, u32[]{:S(2)}) collective-permute-start(bf16[64,2048]{1,0:T(8,128)(2,1)S(1)} %get-tuple-element.647), channel_id=1, source_target_pairs={{8,0},{9,1},{10,2},{11,3},{12,4},{13,5},{14,6},{15,7},{16,8},{17,9... | collective-permute-start | bytes 786440 | tf_op jit(solution)/shard_map/while/body/eval_jaxpr/ppermute | solution.py:14
  803.6 18.0 %collective-permute-start.2 = (bf16[64,2048]{1,0:T(8,128)(2,1)S(1)}, bf16[64,2048]{1,0:T(8,128)(2,1)S(1)}, u32[]{:S(2)}, u32[]{:S(2)}) collective-permute-start(bf16[64,2048]{1,0:T(8,128)(2,1)S(1)} %get-tuple-element.648), channel_id=1, source_target_pairs={{4,0},{5,1},{6,2},{7,3},{8,4},{9,5},{10,6},{11,7},{12,8},{13,9},{1... | collective-permute-start | bytes 786440 | tf_op jit(solution)/shard_map/while/body/eval_jaxpr/ppermute | solution.py:14
  805.5 16.0 %collective-permute-start.3 = (bf16[64,2048]{1,0:T(8,128)(2,1)S(1)}, bf16[64,2048]{1,0:T(8,128)(2,1)S(1)}, u32[]{:S(2)}, u32[]{:S(2)}) collective-permute-start(bf16[64,2048]{1,0:T(8,128)(2,1)S(1)} %get-tuple-element.649), channel_id=1, source_target_pairs={{2,0},{3,1},{4,2},{5,3},{6,4},{7,5},{8,6},{9,7},{10,8},{11,9},{12,... | collective-permute-start | bytes 786440 | tf_op jit(solution)/shard_map/while/body/eval_jaxpr/ppermute | solution.py:14
  808.6 14.9 %collective-permute-start.4 = (bf16[64,2048]{1,0:T(8,128)(2,1)S(1)}, bf16[64,2048]{1,0:T(8,128)(2,1)S(1)}, u32[]{:S(2)}, u32[]{:S(2)}) collective-permute-start(bf16[64,2048]{1,0:T(8,128)(2,1)S(1)} %get-tuple-element.651), channel_id=1, source_target_pairs={{1,0},{2,1},{3,2},{4,3},{5,4},{6,5},{7,6},{8,7},{9,8},{10,9},{11,1... | collective-permute-start | bytes 786440 | tf_op jit(solution)/shard_map/while/body/eval_jaxpr/ppermute | solution.py:14
  863.7 18.4 %collective-permute-start = (bf16[64,2048]{1,0:T(8,128)(2,1)S(1)}, bf16[64,2048]{1,0:T(8,128)(2,1)S(1)}, u32[]{:S(2)}, u32[]{:S(2)}) collective-permute-start(bf16[64,2048]{1,0:T(8,128)(2,1)S(1)} %get-tuple-element.646), channel_id=1, source_target_pairs={{16,0},{17,1},{18,2},{19,3},{20,4},{21,5},{22,6},{23,7},{24,8},{25... | collective-permute-start | bytes 786440 | tf_op jit(solution)/shard_map/while/body/eval_jaxpr/ppermute | solution.py:14
  865.1 22.7 %collective-permute-start.1 = (bf16[64,2048]{1,0:T(8,128)(2,1)S(1)}, bf16[64,2048]{1,0:T(8,128)(2,1)S(1)}, u32[]{:S(2)}, u32[]{:S(2)}) collective-permute-start(bf16[64,2048]{1,0:T(8,128)(2,1)S(1)} %get-tuple-element.647), channel_id=1, source_target_pairs={{8,0},{9,1},{10,2},{11,3},{12,4},{13,5},{14,6},{15,7},{16,8},{17,9... | collective-permute-start | bytes 786440 | tf_op jit(solution)/shard_map/while/body/eval_jaxpr/ppermute | solution.py:14
  867.0 20.8 %collective-permute-start.2 = (bf16[64,2048]{1,0:T(8,128)(2,1)S(1)}, bf16[64,2048]{1,0:T(8,128)(2,1)S(1)}, u32[]{:S(2)}, u32[]{:S(2)}) collective-permute-start(bf16[64,2048]{1,0:T(8,128)(2,1)S(1)} %get-tuple-element.648), channel_id=1, source_target_pairs={{4,0},{5,1},{6,2},{7,3},{8,4},{9,5},{10,6},{11,7},{12,8},{13,9},{1... | collective-permute-start | bytes 786440 | tf_op jit(solution)/shard_map/while/body/eval_jaxpr/ppermute | solution.py:14
  869.0 18.9 %collective-permute-start.3 = (bf16[64,2048]{1,0:T(8,128)(2,1)S(1)}, bf16[64,2048]{1,0:T(8,128)(2,1)S(1)}, u32[]{:S(2)}, u32[]{:S(2)}) collective-permute-start(bf16[64,2048]{1,0:T(8,128)(2,1)S(1)} %get-tuple-element.649), channel_id=1, source_target_pairs={{2,0},{3,1},{4,2},{5,3},{6,4},{7,5},{8,6},{9,7},{10,8},{11,9},{12,... | collective-permute-start | bytes 786440 | tf_op jit(solution)/shard_map/while/body/eval_jaxpr/ppermute | solution.py:14
  872.1 15.7 %collective-permute-start.4 = (bf16[64,2048]{1,0:T(8,128)(2,1)S(1)}, bf16[64,2048]{1,0:T(8,128)(2,1)S(1)}, u32[]{:S(2)}, u32[]{:S(2)}) collective-permute-start(bf16[64,2048]{1,0:T(8,128)(2,1)S(1)} %get-tuple-element.651), channel_id=1, source_target_pairs={{1,0},{2,1},{3,2},{4,3},{5,4},{6,5},{7,6},{8,7},{9,8},{10,9},{11,1... | collective-permute-start | bytes 786440 | tf_op jit(solution)/shard_map/while/body/eval_jaxpr/ppermute | solution.py:14
  (98 other events, 1475.7 us)
Sparse Core Ops, SparseCore 0:
  917.9 108.3 reduce-scatter.1
